TPU v7x, 256 devices: a whole 4x4x8 slice. The times are simulated.
256 devices in a mesh: dp: 32 (over x, z), head: 8 (over y, core).
Axes of the slice: x: 4, y: 4, z: 8, core: 2. Of those that a mesh axis runs over, the one named last changes fastest.
Arguments:
- tokens: bfloat16 [16384, 4096], P('dp'), may hold values from -6 to 6
- q_weight: bfloat16 [4096, 8192], P('dp', 'head'), may hold values from -0.09375 to 0.09375
- kv_weight: bfloat16 [4096, 1024], P('dp', 'head'), may hold values from -0.09375 to 0.09375
- q_gain: float32 [128], replicated, may hold values from 0.1 to 1.9
- k_gain: float32 [128], replicated, may hold values from 0.1 to 1.9
- doc_lengths: int32 [32, 16], replicated, may hold values from 0 to 512, as said below
Outputs:
- attended: bfloat16 [16384, 8192], P('dp', 'head')
Inputs may be any that keep to these rules, and one draw needn't show every extreme that they name: `doc_lengths`: row r lists the lengths of the documents packed in order on index r of dp and sums to 512; some rank holds a single document of 512 tokens.
All inputs are finite; a program needn't handle non-finite values.
Results may differ from a plain program's by a relative error of at most 0.0068.
Values may be sent and summed in bfloat16 or wider, within the bound.
A program may use at most 64 MiB of HBM per device.

v0:
```python
import math
import jax
import jax.numpy as jnp
from jax import lax
from jax.sharding import PartitionSpec as P

KVH = 4
HD = 128
theta_base = 1000000.0
norm_eps = 1e-06


def doc_layout(lengths, count):
    doc_ends = jnp.cumsum(lengths)
    places = jnp.arange(count, dtype=jnp.int32)
    passed = (places[:, None] >= doc_ends[None, :]).astype(jnp.int32)
    doc_ids = jnp.sum(passed, axis=1)
    starts = jnp.sum(passed * lengths[None, :], axis=1)
    return (doc_ids, places - starts)


def norm_rope(raw, gain, positions):
    half_width = raw.shape[-1] // 2
    inv_rms = lax.rsqrt(jnp.mean(raw * raw, axis=-1, keepdims=True) + norm_eps)
    normed = raw * inv_rms * gain
    frequency = jnp.exp(
        jnp.arange(half_width, dtype=jnp.float32) * (-2.0 * math.log(theta_base) / raw.shape[-1])
    )
    angles = positions.astype(jnp.float32)[:, None] * frequency[None, :]
    cosine = jnp.cos(angles)[:, None, :]
    sine_table = jnp.sin(angles)[:, None, :]
    lower_half = normed[..., :half_width]
    second = normed[..., half_width:]
    return jnp.concatenate(
        [lower_half * cosine - second * sine_table, second * cosine + lower_half * sine_table],
        axis=-1,
    ).astype(jnp.bfloat16)


def shards(tokens, q_weight, kv_weight, q_gain, k_gain, doc_lengths):
    rows_here = tokens.shape[0]
    heads_here = q_weight.shape[1] // HD
    own_rank = lax.axis_index("dp")
    kv_all = lax.all_gather(kv_weight, "head", axis=1, tiled=True)
    kv_head = lax.axis_index("head") * KVH // lax.axis_size("head")
    key_cols = lax.dynamic_slice_in_dim(kv_all, kv_head * HD, HD, 1)
    value_cols = lax.dynamic_slice_in_dim(kv_all, (KVH + kv_head) * HD, HD, 1)
    pair_cols = jnp.concatenate([key_cols, value_cols], axis=1)

    def add_rows(shard_rows):
        return jnp.dot(tokens, shard_rows, preferred_element_type=jnp.float32)

    q_sum = add_rows(lax.all_gather(q_weight, "dp", axis=0, tiled=True))
    pair_sum = add_rows(lax.all_gather(pair_cols, "dp", axis=0, tiled=True))
    lengths = lax.dynamic_index_in_dim(doc_lengths, own_rank, 0, keepdims=False)
    doc_ids, positions = doc_layout(lengths, rows_here)
    places = jnp.arange(rows_here, dtype=jnp.int32)
    queries = norm_rope(q_sum.reshape(rows_here, heads_here, HD), q_gain, positions)
    key_rows = norm_rope(pair_sum[:, :HD].reshape(rows_here, 1, HD), k_gain, positions)[:, 0]
    values = pair_sum[:, HD:].astype(jnp.bfloat16)
    scores = jnp.einsum(
        "qhd,td->hqt", queries, key_rows, preferred_element_type=jnp.float32
    ) * HD ** (-0.5)
    allowed = (doc_ids[:, None] == doc_ids[None, :]) & (places[:, None] >= places[None, :])
    weights = jnp.where(allowed[None], jnp.exp(scores), 0.0)
    probs = (weights / jnp.sum(weights, axis=-1, keepdims=True)).astype(jnp.bfloat16)
    mixed_out = jnp.einsum("hqt,td->qhd", probs, values, preferred_element_type=jnp.float32)
    return mixed_out.astype(jnp.bfloat16).reshape(rows_here, heads_here * HD)


def solution(mesh):
    placed = (P("dp", None), P("dp", "head"), P("dp", "head"), P(), P(), P())
    return jax.shard_map(
        shards, mesh=mesh, in_specs=placed, out_specs=P("dp", "head"), check_vma=False
    )
```

profile of v0, /device:TPU:1, one launch (start us, length us, event | category | flops | bytes accessed | tf_op | source)
XLA Modules:
  0.0 222.3 jit_solution(3711025355796249315)
XLA Ops:
  6.5 14.7 %all_gather.9 = bf16[128,1024]{1,0:T(8,128)(2,1)S(1)} all-gather(bf16[128,128]{1,0:T(8,128)(2,1)} %param.8), channel_id=1, replica_groups=mesh['dp'=32,'head'=8] {'head'}, dimensions={1}, use_global_device_ids=true | all-gather | bytes 294912 | tf_op jit(solution)/shard_map/all_gather | solution.py:44
  21.3 0.6 pad_maximum_fusion
  22.0 0.0 all-gather.5.cloned.1.call-start
  22.0 0.7 all-gather.5.cloned.1.call-update
  22.7 0.9 dynamic-slice_reduce_fusion
  23.6 0.1 reduce.2
  23.8 0.1 convert_reduce_fusion
  23.9 0.9 fusion.8
  24.8 1.0 multiply_cosine_fusion
  25.8 70.1 %all-gather.3.cloned.1.call-done = bf16[4096,256]{1,0:T(8,128)(2,1)} async-done(((bf16[128,256]{1,0:T(8,128)(2,1)}), bf16[4096,256]{1,0:T(8,128)(2,1)}) %all-gather.3.cloned.1.call-update) | async-done | bytes 2097168 | tf_op jit(solution)/shard_map/all_gather | solution.py:54
  95.9 4.1 %convolution_bitcast_fusion = f32[512,256]{0,1:T(8,128)S(1)} fusion(bf16[4096,256]{1,0:T(8,128)(2,1)} %all-gather.3.cloned.1.call-done, bf16[512,4096]{1,0:T(8,128)(2,1)} %param.6), kind=kOutput, calls=%fused_computation.10 | convolution fusion | flops 1073741824 | bytes 6815744 | tf_op jit(solution)/shard_map/dot_general | solution.py:51
  100.1 0.1 multiply_bitcast_fusion
  100.2 0.6 fusion.22
  100.7 96.7 %all-gather.5.cloned.1.call-done = bf16[4096,1024]{1,0:T(8,128)(2,1)} async-done(((bf16[128,1024]{1,0:T(8,128)(2,1)}), bf16[4096,1024]{1,0:T(8,128)(2,1)}) %all-gather.5.cloned.1.call-update) | async-done | bytes 8388624 | tf_op jit(solution)/shard_map/all_gather | solution.py:53
  197.4 8.1 %fusion.26 = f32[512,1024]{1,0:T(8,128)S(1)} fusion(bf16[512,4096]{1,0:T(8,128)(2,1)} %param.6, bf16[4096,1024]{1,0:T(8,128)(2,1)} %all-gather.5.cloned.1.call-done), kind=kOutput, calls=%fused_computation.53 | convolution fusion | flops 4294967296 | bytes 14680064 | tf_op jit(solution)/shard_map/dot_general | solution.py:51
  205.6 0.5 copy.39
  206.1 0.6 multiply_reduce_fusion
  206.7 0.1 copy.30
  206.8 1.4 fusion.2
  208.2 0.8 subtract_convert_fusion
  209.0 0.2 copy-done
  209.1 2.6 %fusion = (f32[8,512]{1,0:T(8,128)S(1)}, f32[512,512,8]{1,0,2:T(8,128)S(1)}) fusion(pred[512,512]{0,1:T(8,128)(4,1)S(1)} %copy-done, bf16[512,8,64]{2,0,1:T(8,128)(2,1)S(1)} %get-tuple-element.8, bf16[512,8,64]{2,0,1:T(8,128)(2,1)S(1)} %get-tuple-element.7, bf16[512,64]{0,1:T(8,128)(2,1)S(1)} %get-tuple-element.10, bf16[512,64]{0,1:T(8,128)(2,1)S(1)} %get-tuple-element.9), kind=kOutput, calls=%fused_computation.2 | convolution fusion | flops 545517568 | bytes 9846784 | tf_op jit(solution)/shard_map/qhd,td->hqt/dot_general | solution.py:61
  211.7 2.4 %fusion.3 = bf16[128,8,512]{2,0,1:T(8,128)(2,1)S(1)} fusion(f32[512,512,8]{1,0,2:T(8,128)S(1)} %get-tuple-element.18, f32[8,512]{1,0:T(8,128)S(1)} %get-tuple-element.17, pred[512,512]{0,1:T(8,128)(4,1)S(1)} %copy-done, f32[512,256]{0,1:T(8,128)S(1)} %convolution_bitcast_fusion), kind=kOutput, calls=%fused_computation.9 | convolution fusion | flops 545783808 | bytes 9846784 | tf_op jit(solution)/shard_map/hqt,td->qhd/dot_general | solution.py:67
  214.1 1.3 copy.34
  (12 shorter events, 0.2 us)
Async XLA Ops:
  6.5 89.3 %all-gather.3.cloned.1.call-start = ((), (), s32[]{:S(2)}) async-start(), calls=%async_computation | async-start | bytes 2162688 | tf_op jit(solution)/shard_map/all_gather | solution.py:54
  22.0 175.5 %all-gather.5.cloned.1.call-start = ((), (), s32[]{:S(2)}) async-start(), calls=%async_computation.1 | async-start | bytes 8650752 | tf_op jit(solution)/shard_map/all_gather | solution.py:53
  25.8 74.3 %copy-start.1 = (f32[128]{0:T(128)S(1)}, f32[128]{0:T(128)}, u32[]{:S(2)}) copy-start(f32[128]{0:T(128)} %param.10) | copy-start | bytes 1540
  208.2 1.0 copy-start
Sparse Core Ops, SparseCore 0:
  22.1 73.7 all-gather.2
  98.5 98.9 all-gather.4
where the time goes:
time: 222 us
  waiting for transfers between devices  168 us (76%)
  matrix products  17.3 us (8%)
  blocking collectives  14.7 us (7%)
  between operations  13.5 us (6%)
  other arithmetic  6.22 us (3%)
  local copies, waits for them, and re-layouts  2.96 us (1%)
    all_gather x1, waiting for transfers between devices, shards(): q_sum = add_rows(lax.all_gather(q_weight, 'dp', axis=0, tiled=True))  96.7 us
    all_gather x1, waiting for transfers between devices, shards(): pair_sum = add_rows(lax.all_gather(pair_cols, 'dp', axis=0, tiled=True))  70.1 us
    all_gather x1, blocking collectives, shards(): kv_all = lax.all_gather(kv_weight, 'head', axis=1, tiled=True)  14.7 us
    dot_general x2, matrix products, add_rows(): return jnp.dot(tokens, shard_rows, preferred_element_type=jnp.float32)  12.3 us
  transfers between devices with their start and end apart: 2, of which 2 were waited for; matrix products, arithmetic and copies ran while one was open for 4% of the time, Pallas kernels for 0%

commit v1 on v0

--- a/solution.py
+++ b/solution.py
@@ -41,7 +41,7 @@
     rows_here = tokens.shape[0]
     heads_here = q_weight.shape[1] // HD
     own_rank = lax.axis_index("dp")
-    kv_all = lax.all_gather(kv_weight, "head", axis=1, tiled=True)
+    kv_all = jnp.concatenate(lax.all_gather(kv_weight, "head"), axis=1)
     kv_head = lax.axis_index("head") * KVH // lax.axis_size("head")
     key_cols = lax.dynamic_slice_in_dim(kv_all, kv_head * HD, HD, 1)
     value_cols = lax.dynamic_slice_in_dim(kv_all, (KVH + kv_head) * HD, HD, 1)

time: 222 us -> 223 us (level)
    all_gather x1, waiting for transfers between devices: 70.1 us -> 67.8 us  [shards(): pair_sum = add_rows(lax.all_gather(pair_cols, 'dp', axis=0, tiled=True))]
where the time goes in v1:
time: 223 us; the launch traced here: 222 us
  waiting for transfers between devices  166 us (74%)
  matrix products  17.2 us (8%)
  blocking collectives  16.1 us (7%)
  between operations  13.6 us (6%)
  other arithmetic  6.22 us (3%)
  local copies, waits for them, and re-layouts  3.13 us (1%)
    all_gather x1, waiting for transfers between devices, shards(): q_sum = add_rows(lax.all_gather(q_weight, 'dp', axis=0, tiled=True))  97.7 us
    all_gather x1, waiting for transfers between devices, shards(): pair_sum = add_rows(lax.all_gather(pair_cols, 'dp', axis=0, tiled=True))  67.8 us
    all_gather x1, blocking collectives, shards(): kv_all = jnp.concatenate(lax.all_gather(kv_weight, 'head'), axis=1)  16.1 us
    dot_general x2, matrix products, add_rows(): return jnp.dot(tokens, shard_rows, preferred_element_type=jnp.float32)  12.2 us
  transfers between devices with their start and end apart: 2, of which 2 were waited for; matrix products, arithmetic and copies ran while one was open for 4% of the time, Pallas kernels for 0%

profile of v1, /device:TPU:1, one launch (start us, length us, event | category | flops | bytes accessed | tf_op | source)
XLA Modules:
  0.0 222.5 jit_solution(8465692791971685948)
XLA Ops:
  6.5 16.1 %all-gather = bf16[1024,128]{1,0:T(8,128)(2,1)S(1)} all-gather(bf16[128,128]{1,0:T(8,128)(2,1)} %param.8), channel_id=2, replica_groups=mesh['dp'=32,'head'=8] {'head'}, dimensions={0}, use_global_device_ids=true | all-gather | bytes 294912 | tf_op jit(solution)/shard_map/all_gather | solution.py:44
  22.6 0.2 copy.37
  22.8 0.6 pad_maximum_fusion
  23.5 0.7 all-gather.6.cloned.1.call-update
  24.2 0.9 dynamic-slice_reduce_fusion
  25.1 0.1 reduce.2
  25.3 0.1 convert_reduce_fusion
  25.4 0.9 fusion.8
  26.3 1.0 multiply_cosine_fusion
  27.3 67.8 %all-gather.4.cloned.1.call-done = bf16[4096,256]{0,1:T(8,128)(2,1)} async-done(((bf16[128,256]{0,1:T(8,128)(2,1)}), bf16[4096,256]{0,1:T(8,128)(2,1)}) %all-gather.4.cloned.1.call-update) | async-done | bytes 2097168 | tf_op jit(solution)/shard_map/all_gather | solution.py:54
  95.1 4.1 %convolution_bitcast_fusion = f32[512,256]{0,1:T(8,128)S(1)} fusion(bf16[4096,256]{0,1:T(8,128)(2,1)} %all-gather.4.cloned.1.call-done, bf16[512,4096]{1,0:T(8,128)(2,1)} %param.6), kind=kOutput, calls=%fused_computation.10 | convolution fusion | flops 1073741824 | bytes 6815744 | tf_op jit(solution)/shard_map/dot_general | solution.py:51
  99.2 0.1 multiply_bitcast_fusion
  99.3 0.6 fusion.22
  99.9 97.7 %all-gather.6.cloned.1.call-done = bf16[4096,1024]{1,0:T(8,128)(2,1)} async-done(((bf16[128,1024]{1,0:T(8,128)(2,1)}), bf16[4096,1024]{1,0:T(8,128)(2,1)}) %all-gather.6.cloned.1.call-update) | async-done | bytes 8388624 | tf_op jit(solution)/shard_map/all_gather | solution.py:53
  197.6 8.1 %fusion.26 = f32[512,1024]{1,0:T(8,128)S(1)} fusion(bf16[512,4096]{1,0:T(8,128)(2,1)} %param.6, bf16[4096,1024]{1,0:T(8,128)(2,1)} %all-gather.6.cloned.1.call-done), kind=kOutput, calls=%fused_computation.53 | convolution fusion | flops 4294967296 | bytes 14680064 | tf_op jit(solution)/shard_map/dot_general | solution.py:51
  205.8 0.5 copy.48
  206.3 0.6 multiply_reduce_fusion
  206.9 0.1 copy.39
  207.0 1.4 fusion.2
  208.4 0.8 subtract_convert_fusion
  209.1 0.2 copy-done
  209.3 2.6 %fusion = (f32[8,512]{1,0:T(8,128)S(1)}, f32[512,512,8]{1,0,2:T(8,128)S(1)}) fusion(pred[512,512]{0,1:T(8,128)(4,1)S(1)} %copy-done, bf16[512,8,64]{2,0,1:T(8,128)(2,1)S(1)} %get-tuple-element.8, bf16[512,8,64]{2,0,1:T(8,128)(2,1)S(1)} %get-tuple-element.7, bf16[512,64]{0,1:T(8,128)(2,1)S(1)} %get-tuple-element.10, bf16[512,64]{0,1:T(8,128)(2,1)S(1)} %get-tuple-element.9), kind=kOutput, calls=%fused_computation.2 | convolution fusion | flops 545517568 | bytes 9846784 | tf_op jit(solution)/shard_map/qhd,td->hqt/dot_general | solution.py:61
  211.9 2.4 %fusion.3 = bf16[128,8,512]{2,0,1:T(8,128)(2,1)S(1)} fusion(f32[512,512,8]{1,0,2:T(8,128)S(1)} %get-tuple-element.18, f32[8,512]{1,0:T(8,128)S(1)} %get-tuple-element.17, pred[512,512]{0,1:T(8,128)(4,1)S(1)} %copy-done, f32[512,256]{0,1:T(8,128)S(1)} %convolution_bitcast_fusion), kind=kOutput, calls=%fused_computation.9 | convolution fusion | flops 545783808 | bytes 9846784 | tf_op jit(solution)/shard_map/hqt,td->qhd/dot_general | solution.py:67
  214.3 1.3 copy.43
  (13 shorter events, 0.2 us)
Async XLA Ops:
  6.5 88.5 %all-gather.4.cloned.1.call-start = ((), (), s32[]{:S(2)}) async-start(), calls=%async_computation | async-start | bytes 2162688 | tf_op jit(solution)/shard_map/all_gather | solution.py:54
  23.5 174.2 %all-gather.6.cloned.1.call-start = ((), (), s32[]{:S(2)}) async-start(), calls=%async_computation.1 | async-start | bytes 8650752 | tf_op jit(solution)/shard_map/all_gather | solution.py:53
  27.3 72.0 %copy-start.1 = (f32[128]{0:T(128)S(1)}, f32[128]{0:T(128)}, u32[]{:S(2)}) copy-start(f32[128]{0:T(128)} %param.10) | copy-start | bytes 1540
  208.4 1.0 copy-start
Sparse Core Ops, SparseCore 0:
  23.6 71.4 all-gather.3
  97.7 99.9 all-gather.5

commit v2 on v0

--- a/solution.py
+++ b/solution.py
@@ -51,7 +51,11 @@
         return jnp.dot(tokens, shard_rows, preferred_element_type=jnp.float32)
 
     q_sum = add_rows(lax.all_gather(q_weight, "dp", axis=0, tiled=True))
-    pair_sum = add_rows(lax.all_gather(pair_cols, "dp", axis=0, tiled=True))
+    pair_sum = add_rows(
+        jnp.concatenate(
+            lax.all_to_all(jnp.stack([pair_cols] * lax.axis_size("dp")), "dp", 0, 0), axis=0
+        )
+    )
     lengths = lax.dynamic_index_in_dim(doc_lengths, own_rank, 0, keepdims=False)
     doc_ids, positions = doc_layout(lengths, rows_here)
     places = jnp.arange(rows_here, dtype=jnp.int32)

time: 222 us -> 154 us (0.69)
  waiting for transfers between devices: 168 us -> 89.2 us
  starting transfers between devices: 0.04 us -> 10.4 us
    all_gather x1 -> x0, waiting for transfers between devices: 70.1 us -> none  [shards(): pair_sum = add_rows(lax.all_gather(pair_cols, 'dp', axis=0, tiled=True))]
    all_gather x1, waiting for transfers between devices: 96.7 us -> 34.6 us  [shards(): q_sum = add_rows(lax.all_gather(q_weight, 'dp', axis=0, tiled=True))]
    all_to_all x0 -> x1, waiting for transfers between devices: none -> 53.9 us  [shards(): lax.all_to_all(jnp.stack([pair_cols] * lax.axis_size('dp')), 'dp', 0, 0)]
    all_to_all x0 -> x1, starting transfers between devices: none -> 10.4 us  [shards(): lax.all_to_all(jnp.stack([pair_cols] * lax.axis_size('dp')), 'dp', 0, 0)]
  transfers between devices with their start and end apart: 2 -> 2, of which waited for: 2 -> 2; matrix products, arithmetic and copies ran while one was open for 4% -> 5% of each run, Pallas kernels for 0% -> 0%
where the time goes in v2:
time: 154 us
  waiting for transfers between devices  89.2 us (58%)
  matrix products  16.8 us (11%)
  blocking collectives  14.8 us (10%)
  between operations  13.6 us (9%)
  starting transfers between devices  10.4 us (7%)
  other arithmetic  5.61 us (4%)
  local copies, waits for them, and re-layouts  3.88 us (3%)
    all_to_all x1, waiting for transfers between devices, shards(): lax.all_to_all(jnp.stack([pair_cols] * lax.axis_size('dp')), 'dp', 0, 0)  53.9 us
    all_gather x1, waiting for transfers between devices, shards(): q_sum = add_rows(lax.all_gather(q_weight, 'dp', axis=0, tiled=True))  34.6 us
    all_gather x1, blocking collectives, shards(): kv_all = lax.all_gather(kv_weight, 'head', axis=1, tiled=True)  14.8 us
    dot_general x2, matrix products, add_rows(): return jnp.dot(tokens, shard_rows, preferred_element_type=jnp.float32)  11.8 us
    all_to_all x1, starting transfers between devices, shards(): lax.all_to_all(jnp.stack([pair_cols] * lax.axis_size('dp')), 'dp', 0, 0)  10.4 us
  transfers between devices with their start and end apart: 2, of which 2 were waited for; matrix products, arithmetic and copies ran while one was open for 5% of the time, Pallas kernels for 0%

profile of v2, /device:TPU:1, one launch (start us, length us, event | category | flops | bytes accessed | tf_op | source)
XLA Modules:
  0.0 154.1 jit_solution(7735997187888704100)
XLA Ops:
  6.5 0.7 all-gather.2.cloned.1.call-update
  7.3 14.8 %all_gather.6 = bf16[128,1024]{1,0:T(8,128)(2,1)S(1)} all-gather(bf16[128,128]{1,0:T(8,128)(2,1)} %param.8), channel_id=1, replica_groups=mesh['dp'=32,'head'=8] {'head'}, dimensions={1}, use_global_device_ids=true | all-gather | bytes 294912 | tf_op jit(solution)/shard_map/all_gather | solution.py:44
  22.1 1.6 %stack.2 = bf16[32,128,256]{2,1,0:T(8,128)(2,1)} broadcast(bf16[128,256]{1,0:T(8,128)(2,1)S(1)} %pad_maximum_fusion), dimensions={1,2} | broadcast | bytes 2162688 | tf_op jit(solution)/shard_map/stack | solution.py:56
  23.7 10.4 %all-to-all-start = ((bf16[32,128,256]{2,1,0:T(8,128)(2,1)}), bf16[32,128,256]{2,1,0:T(8,128)(2,1)S(1)}, u32[]{:S(2)}, u32[]{:S(2)}) async-start(bf16[32,128,256]{2,1,0:T(8,128)(2,1)} %stack.2), calls=%async_computation | async-start | bytes 4194304 | tf_op jit(solution)/shard_map/all_to_all | solution.py:56
  34.1 0.2 dynamic-slice_reduce_fusion
  34.3 0.1 reduce.2
  34.4 0.1 convert_reduce_fusion
  34.6 0.9 fusion.8
  35.5 1.0 multiply_cosine_fusion
  36.5 53.9 %all-to-all-done = bf16[32,128,256]{2,1,0:T(8,128)(2,1)S(1)} async-done(((bf16[32,128,256]{2,1,0:T(8,128)(2,1)}), bf16[32,128,256]{2,1,0:T(8,128)(2,1)S(1)}, u32[]{:S(2)}, u32[]{:S(2)}) %all-to-all-start) | async-done | bytes 2097184 | tf_op jit(solution)/shard_map/all_to_all | solution.py:56
  90.3 3.6 %convolution_bitcast_fusion = f32[512,256]{0,1:T(8,128)S(1)} fusion(bf16[4096,256]{1,0:T(8,128)(2,1)S(1)} %bitcast.46, bf16[512,4096]{1,0:T(8,128)(2,1)} %param.6), kind=kOutput, calls=%fused_computation.10 | convolution fusion | flops 1073741824 | bytes 6815744 | tf_op jit(solution)/shard_map/dot_general | solution.py:51
  94.0 0.1 multiply_bitcast_fusion
  94.1 0.6 fusion.22
  94.7 34.6 %all-gather.2.cloned.1.call-done = bf16[4096,1024]{1,0:T(8,128)(2,1)} async-done(((bf16[128,1024]{1,0:T(8,128)(2,1)}), bf16[4096,1024]{1,0:T(8,128)(2,1)}) %all-gather.2.cloned.1.call-update) | async-done | bytes 8388624 | tf_op jit(solution)/shard_map/all_gather | solution.py:53
  129.3 8.1 %fusion.26 = f32[512,1024]{1,0:T(8,128)S(1)} fusion(bf16[512,4096]{1,0:T(8,128)(2,1)} %param.6, bf16[4096,1024]{1,0:T(8,128)(2,1)} %all-gather.2.cloned.1.call-done), kind=kOutput, calls=%fused_computation.53 | convolution fusion | flops 4294967296 | bytes 14680064 | tf_op jit(solution)/shard_map/dot_general | solution.py:51
  137.4 0.5 copy.39
  137.9 0.6 multiply_reduce_fusion
  138.5 0.1 copy.30
  138.6 1.4 fusion.2
  140.0 0.8 subtract_convert_fusion
  140.8 0.2 copy-done
  140.9 2.6 %fusion = (f32[8,512]{1,0:T(8,128)S(1)}, f32[512,512,8]{1,0,2:T(8,128)S(1)}) fusion(pred[512,512]{0,1:T(8,128)(4,1)S(1)} %copy-done, bf16[512,8,64]{2,0,1:T(8,128)(2,1)S(1)} %get-tuple-element.8, bf16[512,8,64]{2,0,1:T(8,128)(2,1)S(1)} %get-tuple-element.7, bf16[512,64]{0,1:T(8,128)(2,1)S(1)} %get-tuple-element.10, bf16[512,64]{0,1:T(8,128)(2,1)S(1)} %get-tuple-element.9), kind=kOutput, calls=%fused_computation.2 | convolution fusion | flops 545517568 | bytes 9846784 | tf_op jit(solution)/shard_map/qhd,td->hqt/dot_general | solution.py:65
  143.6 2.4 %fusion.3 = bf16[128,8,512]{2,0,1:T(8,128)(2,1)S(1)} fusion(f32[512,512,8]{1,0,2:T(8,128)S(1)} %get-tuple-element.18, f32[8,512]{1,0:T(8,128)S(1)} %get-tuple-element.17, pred[512,512]{0,1:T(8,128)(4,1)S(1)} %copy-done, f32[512,256]{0,1:T(8,128)S(1)} %convolution_bitcast_fusion), kind=kOutput, calls=%fused_computation.9 | convolution fusion | flops 545783808 | bytes 9846784 | tf_op jit(solution)/shard_map/hqt,td->qhd/dot_general | solution.py:71
  146.0 1.3 copy.34
  (14 shorter events, 0.2 us)
Async XLA Ops:
  6.5 122.7 %all-gather.2.cloned.1.call-start = ((), (), s32[]{:S(2)}) async-start(), calls=%async_computation.1 | async-start | bytes 8650752 | tf_op jit(solution)/shard_map/all_gather | solution.py:53
  23.7 10.4 %copy-start.1 = (s32[32,16]{0,1:T(8,128)S(1)}, s32[32,16]{0,1:T(8,128)}, u32[]{:S(2)}) copy-start(s32[32,16]{0,1:T(8,128)} %param.11) | copy-start | bytes 6148
  23.7 66.6 %all-to-all-start = ((bf16[32,128,256]{2,1,0:T(8,128)(2,1)}), bf16[32,128,256]{2,1,0:T(8,128)(2,1)S(1)}, u32[]{:S(2)}, u32[]{:S(2)}) async-start(bf16[32,128,256]{2,1,0:T(8,128)(2,1)} %stack.2), calls=%async_computation | async-start | bytes 4194304 | tf_op jit(solution)/shard_map/all_to_all | solution.py:56
  90.3 3.7 %copy-start.2 = (f32[128]{0:T(128)S(1)}, f32[128]{0:T(128)}, u32[]{:S(2)}) copy-start(f32[128]{0:T(128)} %param.10) | copy-start | bytes 1540
  140.0 1.0 copy-start
Sparse Core Ops, SparseCore 0:
  9.9 119.2 all-gather.1
